TPU v7x, 512 devices: a whole 4x8x8 slice. The times are simulated.
512 devices in a mesh: sub: 64 (over y, z), crow: 4 (over x_lo, core), ccol: 2 (over x_hi).
Axes of the slice: x: 4 (x_hi: 2, x_lo: 2; x = x_hi * 2 + x_lo), y: 8, z: 8, core: 2. Of those that a mesh axis runs over, the one named last changes fastest.
Arguments:
- loads: bfloat16 [128, 1024, 128], P('sub'), may hold values from -6 to 6
- stiffness: bfloat16 [128, 1024, 1024], P('sub', ('crow', 'ccol'))
- local_inverse: bfloat16 [128, 1024, 1024], P('sub', ('crow', 'ccol'))
- coarse_basis: bfloat16 [128, 1024, 48], P('sub', ('crow', 'ccol')), may hold values from -0.1875 to 0.1875
- coarse_inverse: bfloat16 [6144, 6144], P('sub', ('crow', 'ccol'))
- coarse_index: int32 [128, 48], P('sub'), may hold values from 0 to 6143, as said below
- left_rows: int32 [128, 128], P('sub'), may hold values from 0 to 1023, as said below
- right_rows: int32 [128, 128], P('sub'), may hold values from 0 to 1023, as said below
Outputs:
- second_pass: float32 [128, 1024, 128], P('sub', ('crow', 'ccol'))
- final_residual: float32 [128, 1024, 128], P('sub', ('crow', 'ccol'))
Inputs may be any that keep to these rules, and one draw needn't show every extreme that they name: `coarse_index`: every value 0 to 6143 appears exactly once in the whole array. Of the 96 values in the rows of one index of sub, at most 24 lie in one block of 768 consecutive coarse rows starting at a multiple of 768, and that most is reached. In each subdomain the 128 entries of left_rows and the 128 entries of right_rows are 256 distinct rows. `right_rows`: see left_rows.
All inputs are finite; a program needn't handle non-finite values.
Results may differ from a plain program's by a relative error of at most 0.0067.
Values may be sent and summed in bfloat16 or wider, within the bound.
A program may use at most 64 MiB of HBM per device.

v0:
```python
import jax
import jax.numpy as jnp
from jax import lax
from jax.sharding import PartitionSpec as P


def padded(block, sides, width):
    for axis, dim in sides:
        count = lax.axis_size(axis)
        forward = [(i, i + 1) for i in range(count - 1)]
        forward.append((count - 1, 0))
        backward = [(target, source) for source, target in forward]
        low = lax.ppermute(
            lax.slice_in_dim(block, block.shape[dim] - width, None, axis=dim), axis, forward
        )
        high = lax.ppermute(lax.slice_in_dim(block, 0, width, axis=dim), axis, backward)
        block = jnp.concatenate([low, block, high], axis=dim)
    return block


def fold_product(matrix, gathered_piece):
    return jnp.einsum("sij,sjc->sic", matrix, gathered_piece, preferred_element_type=jnp.float32)


def apply_stiffness(iterate, stiffness, pick_left, pick_right):
    sub_count, row_count, case_count = iterate.shape
    rounded = iterate.astype(jnp.bfloat16)
    product = fold_product(stiffness, lax.all_gather(rounded, ("crow", "ccol"), axis=1, tiled=True))
    product_b = product.astype(jnp.bfloat16)
    left_part = jnp.einsum("sfi,sic->sfc", pick_left, product_b, preferred_element_type=jnp.float32)
    right_part = jnp.einsum(
        "sfi,sic->sfc", pick_right, product_b, preferred_element_type=jnp.float32
    )
    partial_faces = jnp.stack([left_part, right_part], axis=1)
    boundary = lax.psum(partial_faces.astype(jnp.bfloat16), ("crow", "ccol"))
    extended = padded(boundary, (("sub", 0),), 1)
    from_before = extended[:sub_count, 1]
    from_after = extended[2:, 0]
    added_left = jnp.einsum(
        "sfi,sfc->sic", pick_left, from_before, preferred_element_type=jnp.float32
    )
    added_right = jnp.einsum(
        "sfi,sfc->sic", pick_right, from_after, preferred_element_type=jnp.float32
    )
    return product_b.astype(jnp.float32) + added_left + added_right


def coarse_step(restricted, coarse_inverse, coarse_index):
    sub_count, mode_count, case_count = restricted.shape
    flat_rows = restricted.reshape(sub_count * mode_count, case_count)
    flat_index = coarse_index.reshape(-1)
    owned_rows, block_width = coarse_inverse.shape
    block_index = lax.axis_index(("crow", "ccol"))
    arrived, arrived_index = (
        lax.all_gather(flat_rows, "sub", axis=0, tiled=True),
        lax.all_gather(flat_index, "sub", axis=0, tiled=True),
    )
    shifted_place = arrived_index - block_index * block_width
    inside = (shifted_place >= 0) & (shifted_place < block_width)
    arrived_place = jnp.where(inside, shifted_place, block_width)
    ordered = (
        jnp.zeros((block_width + 1, case_count), jnp.bfloat16)
        .at[arrived_place]
        .set(arrived)[:block_width]
    )
    partial_coarse = jnp.dot(coarse_inverse, ordered, preferred_element_type=jnp.float32)
    coarse = lax.psum(partial_coarse, ("crow", "ccol")).astype(jnp.bfloat16)
    everything = lax.all_gather(coarse, "sub", axis=0, tiled=True)
    picked = everything[flat_index]
    return picked.reshape(sub_count, mode_count, case_count)


def precondition(local_part, residual_rows, coarse_basis, coarse_inverse, coarse_index):
    partial_modes = jnp.einsum(
        "sik,sic->skc", coarse_basis, residual_rows, preferred_element_type=jnp.float32
    )
    restricted = lax.psum(partial_modes, ("crow", "ccol")).astype(jnp.bfloat16)
    picked = coarse_step(restricted, coarse_inverse, coarse_index)
    return local_part + jnp.einsum(
        "sik,skc->sic", coarse_basis, picked, preferred_element_type=jnp.float32
    )


def body(
    loads,
    stiffness,
    local_inverse,
    coarse_basis,
    coarse_inverse,
    coarse_index,
    left_rows,
    right_rows,
):
    sub_count, row_count, iface_count = stiffness.shape
    group_index = lax.axis_index(("crow", "ccol"))
    first_row = group_index * row_count
    loads_rows = lax.dynamic_slice_in_dim(loads, first_row, row_count, 1)
    local_rows = first_row + jnp.arange(row_count, dtype=jnp.int32)
    pick_left = (left_rows[:, :, None] == local_rows[None, None, :]).astype(jnp.bfloat16)
    pick_right = (right_rows[:, :, None] == local_rows[None, None, :]).astype(jnp.bfloat16)
    first_local = jnp.einsum(
        "sij,sjc->sic", local_inverse, loads, preferred_element_type=jnp.float32
    )
    first_pass = precondition(first_local, loads_rows, coarse_basis, coarse_inverse, coarse_index)
    image_first = apply_stiffness(first_pass, stiffness, pick_left, pick_right)
    residual_b = (loads_rows.astype(jnp.float32) - image_first).astype(jnp.bfloat16)
    second_local = fold_product(
        local_inverse, lax.all_gather(residual_b, ("crow", "ccol"), axis=1, tiled=True)
    )
    second_pass = first_pass + precondition(
        second_local, residual_b, coarse_basis, coarse_inverse, coarse_index
    )
    image_second = apply_stiffness(second_pass, stiffness, pick_left, pick_right)
    final_residual = loads_rows.astype(jnp.float32) - image_second
    return (second_pass, final_residual)


def solution(mesh):
    return jax.shard_map(
        body,
        mesh=mesh,
        in_specs=(
            P("sub", None, None),
            P("sub", ("crow", "ccol"), None),
            P("sub", ("crow", "ccol"), None),
            P("sub", ("crow", "ccol"), None),
            P("sub", ("crow", "ccol")),
            P("sub", None),
            P("sub", None),
            P("sub", None),
        ),
        out_specs=(P("sub", ("crow", "ccol"), None), P("sub", ("crow", "ccol"), None)),
        check_vma=False,
    )
```

profile of v0, /device:TPU:6, one launch (start us, length us, event | category | flops | bytes accessed | tf_op | source)
XLA Modules:
  0.0 929.7 jit_solution(8455041256860478172)
XLA Ops:
  7.2 1.1 convolution_bitcast_fusion.4
  8.3 34.2 %psum.42 = bf16[2,48,128]{2,1,0:T(8,128)(2,1)} all-reduce(f32[2,48,128]{2,1,0:T(8,128)S(1)} %convolution_bitcast_fusion.4), channel_id=1, replica_groups=mesh['sub'=64,'crow'=4,'ccol'=2] {'crow','ccol'}, use_global_device_ids=true, to_apply=%region_0.0 | all-reduce | flops 12288 | bytes 73728 | tf_op jit(solution)/shard_map/psum | solution.py:77
  43.3 1.3 dynamic-slice
  45.6 282.8 %all-reduce = s32[6144]{0:T(1024)S(1)} all-reduce(s32[6144]{0:T(1024)S(1)} %dynamic-update-slice), channel_id=1, replica_groups=mesh['sub'=64,'crow'=4,'ccol'=2] {'sub'}, use_global_device_ids=true, to_apply=%add | all-reduce | flops 6144 | bytes 49152
  328.4 16.2 %scatter_custom_fusion = bf16[769,128]{1,0:T(8,128)(2,1)S(1)} fusion(s32[6144]{0:T(1024)S(1)} %compare_select_fusion, bf16[6144,128]{1,0:T(8,128)(2,1)} %all-gather.5.cloned.1.call-done, bf16[]{:T(256)} %constant.10.clone.1), kind=kCustom, calls=%fused_computation.46 | custom fusion | bytes 197376 | tf_op jit(solution)/shard_map/scatter | solution.py:64
  344.6 1.1 convolution_bitcast_fusion.3
  345.7 30.7 %psum.43 = bf16[96,128]{1,0:T(8,128)(2,1)} all-reduce(f32[96,128]{1,0:T(8,128)S(1)} %convolution_bitcast_fusion.3), channel_id=1, replica_groups=mesh['sub'=64,'crow'=4,'ccol'=2] {'crow','ccol'}, use_global_device_ids=true, to_apply=%region_2.3 | all-reduce | flops 12288 | bytes 73728 | tf_op jit(solution)/shard_map/psum | solution.py:67
  377.2 75.1 %all-gather.7.cloned.1.call-done = bf16[6144,128]{1,0:T(8,128)(2,1)} async-done(((bf16[96,128]{1,0:T(8,128)(2,1)}), bf16[6144,128]{1,0:T(8,128)(2,1)}) %all-gather.7.cloned.1.call-update) | async-done | bytes 1572880 | tf_op jit(solution)/shard_map/all_gather | solution.py:68
  452.4 2.2 gather_fusion
  454.6 0.9 convolution_bitcast_fusion
  455.9 27.2 %all_gather.28 = bf16[2,1024,128]{2,1,0:T(8,128)(2,1)S(1)} all-gather(bf16[2,128,128]{2,1,0:T(8,128)(2,1)S(1)} %get-tuple-element.6), channel_id=1, replica_groups=mesh['sub'=64,'crow'=4,'ccol'=2] {'crow','ccol'}, dimensions={1}, use_global_device_ids=true | all-gather | bytes 589824 | tf_op jit(solution)/shard_map/all_gather | solution.py:28
  484.7 65.4 %all-reduce.4.cloned.1.call-done = bf16[2,2,128,128]{3,2,0,1:T(8,128)(2,1)} async-done(((bf16[2,2,128,128]{3,2,0,1:T(8,128)(2,1)}), bf16[2,2,128,128]{3,2,0,1:T(8,128)(2,1)}) %all-reduce.4.cloned.1.call-update) | async-done | bytes 131088 | tf_op jit(solution)/shard_map/psum | solution.py:35
  550.9 8.1 collective-permute-start.1
  559.1 1.9 collective-permute-start
  561.2 1.0 fusion.14
  562.2 6.5 collective-permute-done
  568.6 1.0 fusion.6
  569.8 30.8 %psum.45 = bf16[2,48,128]{2,1,0:T(8,128)(2,1)} all-reduce(f32[2,48,128]{2,1,0:T(8,128)S(1)} %convolution_bitcast_fusion.2), channel_id=1, replica_groups=mesh['sub'=64,'crow'=4,'ccol'=2] {'crow','ccol'}, use_global_device_ids=true, to_apply=%region_4.5 | all-reduce | flops 12288 | bytes 73728 | tf_op jit(solution)/shard_map/psum | solution.py:77
  600.7 77.5 %all-gather.9.cloned.1.call-done = bf16[6144,128]{1,0:T(8,128)(2,1)} async-done(((bf16[96,128]{1,0:T(8,128)(2,1)}), bf16[6144,128]{1,0:T(8,128)(2,1)}) %all-gather.9.cloned.1.call-update) | async-done | bytes 1572880 | tf_op jit(solution)/shard_map/all_gather | solution.py:55
  678.2 16.2 %scatter_custom_fusion.1 = bf16[769,128]{1,0:T(8,128)(2,1)S(1)} fusion(s32[6144]{0:T(1024)S(1)} %compare_select_fusion, bf16[6144,128]{1,0:T(8,128)(2,1)} %all-gather.9.cloned.1.call-done, bf16[]{:T(256)} %constant.10.clone.1), kind=kCustom, calls=%fused_computation.44 | custom fusion | bytes 197376 | tf_op jit(solution)/shard_map/scatter | solution.py:64
  694.6 30.9 %psum.46 = bf16[96,128]{1,0:T(8,128)(2,1)} all-reduce(f32[96,128]{1,0:T(8,128)S(1)} %convolution_bitcast_fusion.1), channel_id=1, replica_groups=mesh['sub'=64,'crow'=4,'ccol'=2] {'crow','ccol'}, use_global_device_ids=true, to_apply=%region_6.7 | all-reduce | flops 12288 | bytes 73728 | tf_op jit(solution)/shard_map/psum | solution.py:67
  725.6 27.3 %all_gather.29 = bf16[2,1024,128]{2,1,0:T(8,128)(2,1)S(1)} all-gather(bf16[2,128,128]{2,1,0:T(8,128)(2,1)S(1)} %fusion.6), channel_id=1, replica_groups=mesh['sub'=64,'crow'=4,'ccol'=2] {'crow','ccol'}, dimensions={1}, use_global_device_ids=true | all-gather | bytes 589824 | tf_op jit(solution)/shard_map/all_gather | solution.py:108
  752.8 52.2 %all-gather.11.cloned.1.call-done = bf16[6144,128]{1,0:T(8,128)(2,1)} async-done(((bf16[96,128]{1,0:T(8,128)(2,1)}), bf16[6144,128]{1,0:T(8,128)(2,1)}) %all-gather.11.cloned.1.call-update) | async-done | bytes 1572880 | tf_op jit(solution)/shard_map/all_gather | solution.py:68
  805.1 2.2 gather_fusion.1
  807.5 1.0 fusion.65
  808.5 27.2 %all_gather.32 = bf16[2,1024,128]{2,1,0:T(8,128)(2,1)S(1)} all-gather(bf16[2,128,128]{2,1,0:T(8,128)(2,1)S(1)} %get-tuple-element.8), channel_id=1, replica_groups=mesh['sub'=64,'crow'=4,'ccol'=2] {'crow','ccol'}, dimensions={1}, use_global_device_ids=true | all-gather | bytes 589824 | tf_op jit(solution)/shard_map/all_gather | solution.py:28
  837.2 65.4 %all-reduce.6.cloned.1.call-done = bf16[2,2,128,128]{3,2,0,1:T(8,128)(2,1)} async-done(((bf16[2,2,128,128]{3,2,0,1:T(8,128)(2,1)}), bf16[2,2,128,128]{3,2,0,1:T(8,128)(2,1)}) %all-reduce.6.cloned.1.call-update) | async-done | bytes 131088 | tf_op jit(solution)/shard_map/psum | solution.py:35
  903.5 8.1 collective-permute-start.3
  911.6 1.9 collective-permute-start.2
  913.8 1.0 fusion.11
  914.7 6.5 collective-permute-done.2
  921.2 1.6 fusion.3
  (51 shorter events, 8.3 us)
Async XLA Ops:
  7.2 448.4 %copy-start = (bf16[2,128,1024]{2,1,0:T(8,128)(2,1)S(1)}, bf16[2,128,1024]{2,1,0:T(8,128)(2,1)}, u32[]{:S(2)}) copy-start(bf16[2,128,1024]{2,1,0:T(8,128)(2,1)} %param.10) | copy-start | bytes 1572868
  7.2 448.4 %copy-start.2 = (bf16[2,1024,128]{2,1,0:T(8,128)(2,1)S(1)}, bf16[2,1024,128]{2,1,0:T(8,128)(2,1)}, u32[]{:S(2)}) copy-start(bf16[2,1024,128]{2,1,0:T(8,128)(2,1)} %param.8) | copy-start | bytes 1572868
  7.2 321.2 %all-gather.5.cloned.1.call-start = ((), (), s32[]{:S(2)}) async-start(), calls=%async_computation | async-start | bytes 1597440 | tf_op jit(solution)/shard_map/all_gather | solution.py:55
  42.5 409.8 %all-gather.7.cloned.1.call-start = ((), (), s32[]{:S(2)}) async-start(), calls=%async_computation.1 | async-start | bytes 1597440 | tf_op jit(solution)/shard_map/all_gather | solution.py:68
  328.3 154.7 %copy-start.1 = (bf16[2,128,1024]{2,1,0:T(8,128)(2,1)S(1)}, bf16[2,128,1024]{2,1,0:T(8,128)(2,1)}, u32[]{:S(2)}) copy-start(bf16[2,128,1024]{2,1,0:T(8,128)(2,1)} %param.9) | copy-start | bytes 1572868
  376.4 173.7 %all-reduce.4.cloned.1.call-start = ((), (), s32[]{:S(2)}) async-start(), calls=%async_computation.2 | async-start | bytes 262144 | tf_op jit(solution)/shard_map/psum | solution.py:35
  455.6 27.8 %copy-start.5 = (s32[2,128]{1,0:T(2,128)S(1)}, s32[2,128]{1,0:T(2,128)}, u32[]{:S(2)}) copy-start(s32[2,128]{1,0:T(2,128)} %param.15) | copy-start | bytes 3076
  455.6 28.1 %copy-start.6 = (s32[2,128]{1,0:T(2,128)S(1)}, s32[2,128]{1,0:T(2,128)}, u32[]{:S(2)}) copy-start(s32[2,128]{1,0:T(2,128)} %param.14) | copy-start | bytes 3076
  483.1 86.6 %copy-start.4 = (bf16[2,128,48]{1,2,0:T(8,128)(2,1)S(1)}, bf16[2,128,48]{1,2,0:T(8,128)(2,1)}, u32[]{:S(2)}) copy-start(bf16[2,128,48]{1,2,0:T(8,128)(2,1)} %param.11) | copy-start | bytes 73732
  483.1 211.3 %copy-start.3 = (bf16[96,768]{1,0:T(8,128)(2,1)S(1)}, bf16[96,768]{1,0:T(8,128)(2,1)}, u32[]{:S(2)}) copy-start(bf16[96,768]{1,0:T(8,128)(2,1)} %param.12) | copy-start | bytes 442372
  484.7 193.5 %all-gather.9.cloned.1.call-start = ((), (), s32[]{:S(2)}) async-start(), calls=%async_computation.3 | async-start | bytes 1597440 | tf_op jit(solution)/shard_map/all_gather | solution.py:55
  550.9 10.3 %collective-permute-start.1 = (bf16[1,2,128,128]{3,2,0,1:T(8,128)(2,1)S(1)}, bf16[1,2,128,128]{3,2,0,1:T(8,128)(2,1)S(1)}, u32[]{:S(2)}, u32[]{:S(2)}) collective-permute-start(bf16[1,2,128,128]{3,2,0,1:T(8,128)(2,1)S(1)} %get-tuple-element.5), channel_id=1, source_target_pairs={{8,0},{16,8},{24,16},{32,24},{40,32},{48,40},{56,48},{64,56},{72,6... | collective-permute-start | bytes 196616 | tf_op jit(solution)/shard_map/ppermute | solution.py:16
  559.1 9.6 %collective-permute-start = (bf16[1,2,128,128]{3,2,0,1:T(8,128)(2,1)S(1)}, bf16[1,2,128,128]{3,2,0,1:T(8,128)(2,1)S(1)}, u32[]{:S(2)}, u32[]{:S(2)}) collective-permute-start(bf16[1,2,128,128]{3,2,0,1:T(8,128)(2,1)S(1)} %get-tuple-element.4), channel_id=1, source_target_pairs={{0,8},{8,16},{16,24},{24,32},{32,40},{40,48},{48,56},{56,64},{64,7... | collective-permute-start | bytes 196616 | tf_op jit(solution)/shard_map/ppermute | solution.py:13
  600.6 204.4 %all-gather.11.cloned.1.call-start = ((), (), s32[]{:S(2)}) async-start(), calls=%async_computation.4 | async-start | bytes 1597440 | tf_op jit(solution)/shard_map/all_gather | solution.py:68
  725.5 177.1 %all-reduce.6.cloned.1.call-start = ((), (), s32[]{:S(2)}) async-start(), calls=%async_computation.5 | async-start | bytes 262144 | tf_op jit(solution)/shard_map/psum | solution.py:35
  903.5 10.3 %collective-permute-start.3 = (bf16[1,2,128,128]{3,2,0,1:T(8,128)(2,1)S(1)}, bf16[1,2,128,128]{3,2,0,1:T(8,128)(2,1)S(1)}, u32[]{:S(2)}, u32[]{:S(2)}) collective-permute-start(bf16[1,2,128,128]{3,2,0,1:T(8,128)(2,1)S(1)} %get-tuple-element.3), channel_id=1, source_target_pairs={{8,0},{16,8},{24,16},{32,24},{40,32},{48,40},{56,48},{64,56},{72,6... | collective-permute-start | bytes 196616 | tf_op jit(solution)/shard_map/ppermute | solution.py:16
  911.6 9.6 %collective-permute-start.2 = (bf16[1,2,128,128]{3,2,0,1:T(8,128)(2,1)S(1)}, bf16[1,2,128,128]{3,2,0,1:T(8,128)(2,1)S(1)}, u32[]{:S(2)}, u32[]{:S(2)}) collective-permute-start(bf16[1,2,128,128]{3,2,0,1:T(8,128)(2,1)S(1)} %get-tuple-element.2), channel_id=1, source_target_pairs={{0,8},{8,16},{16,24},{24,32},{32,40},{40,48},{48,56},{56,64},{64,7... | collective-permute-start | bytes 196616 | tf_op jit(solution)/shard_map/ppermute | solution.py:13
Sparse Core Ops, SparseCore 0:
  42.7 83.8 all-gather.4
  376.5 75.8 all-gather.6
  484.8 65.2 all-reduce.3
  600.8 77.3 all-gather.8
  725.6 79.3 all-gather.10
  837.3 65.2 all-reduce.5
where the time goes:
time: 931 us; the launch traced here: 930 us
  blocking collectives  491 us (53%)
  waiting for transfers between devices  349 us (37%)
  local copies, waits for them, and re-layouts  41.7 us (4%)
  starting transfers between devices  20.3 us (2%)
  between operations  15 us (2%)
  matrix products  11.1 us (1%)
    unnamed x1, blocking collectives  283 us
    psum x2, waiting for transfers between devices, apply_stiffness(): boundary = lax.psum(partial_faces.astype(jnp.bfloat16), ('crow', 'ccol'))  131 us
    all_gather x2, waiting for transfers between devices, coarse_step(): everything = lax.all_gather(coarse, 'sub', axis=0, tiled=True)  127 us
    all_gather x2, waiting for transfers between devices, coarse_step(): lax.all_gather(flat_rows, 'sub', axis=0, tiled=True)  77.5 us
    psum x2, blocking collectives, precondition(): restricted = lax.psum(partial_modes, ('crow', 'ccol')).astype(jnp.bfloat16)  65 us
    psum x2, blocking collectives, coarse_step(): coarse = lax.psum(partial_coarse, ('crow', 'ccol')).astype(jnp.bfloat16)  61.6 us
    all_gather x2, blocking collectives, apply_stiffness(): lax.all_gather(rounded, ('crow', 'ccol'), axis=1, tiled=True)  54.3 us
    scatter x2, local copies, waits for them, and re-layouts, coarse_step(): ordered = jnp.zeros((block_width + 1, case_count), jnp.bfloat16).at[arriv...  32.4 us
  transfers between devices with their start and end apart: 10, of which 9 were waited for; matrix products, arithmetic and copies ran while one was open for 1% of the time, Pallas kernels for 0%

commit v1 on v0

--- a/solution.py
+++ b/solution.py
@@ -2,6 +2,14 @@
 import jax.numpy as jnp
 from jax import lax
 from jax.sharding import PartitionSpec as P
+
+
+def gather_from_all(shard, axis, dim):
+    size = lax.axis_size(axis)
+    repeats = [size if d == dim else 1 for d in range(shard.ndim)]
+    return lax.all_to_all(
+        jnp.tile(shard, repeats), axis, split_axis=dim, concat_axis=dim, tiled=True
+    )
 
 
 def padded(block, sides, width):
@@ -52,7 +60,7 @@
     owned_rows, block_width = coarse_inverse.shape
     block_index = lax.axis_index(("crow", "ccol"))
     arrived, arrived_index = (
-        lax.all_gather(flat_rows, "sub", axis=0, tiled=True),
+        gather_from_all(flat_rows, "sub", 0),
         lax.all_gather(flat_index, "sub", axis=0, tiled=True),
     )
     shifted_place = arrived_index - block_index * block_width

time: 931 us -> 938 us (level)
  waiting for transfers between devices: 349 us -> 280 us
  blocking collectives: 491 us -> 555 us
  starting transfers between devices: 20.3 us -> 33.7 us
    all_gather x2 -> x0, waiting for transfers between devices: 77.5 us -> none  [coarse_step(): lax.all_gather(flat_rows, 'sub', axis=0, tiled=True)]
    all_to_all x0 -> x1, blocking collectives: none -> 47.2 us  [gather_from_all(): lax.all_to_all(jnp.tile(shard, repeats), axis, split_axis=dim, concat_axi...]
    unnamed x1, blocking collectives: 283 us -> 301 us
    all_to_all x0 -> x1, starting transfers between devices: none -> 13.4 us  [gather_from_all(): lax.all_to_all(jnp.tile(shard, repeats), axis, split_axis=dim, concat_axi...]
  transfers between devices with their start and end apart: 10 -> 9, of which waited for: 9 -> 8; matrix products, arithmetic and copies ran while one was open for 1% -> 0% of each run, Pallas kernels for 0% -> 0%
where the time goes in v1:
time: 938 us; the launch traced here: 937 us
  blocking collectives  555 us (59%)
  waiting for transfers between devices  280 us (30%)
  local copies, waits for them, and re-layouts  42.1 us (4%)
  starting transfers between devices  33.7 us (4%)
  between operations  14.7 us (2%)
  matrix products  10.1 us (1%)
    unnamed x1, blocking collectives  301 us
    all_gather x2, waiting for transfers between devices, coarse_step(): everything = lax.all_gather(coarse, 'sub', axis=0, tiled=True)  136 us
    psum x2, waiting for transfers between devices, apply_stiffness(): boundary = lax.psum(partial_faces.astype(jnp.bfloat16), ('crow', 'ccol'))  131 us
    psum x2, blocking collectives, precondition(): restricted = lax.psum(partial_modes, ('crow', 'ccol')).astype(jnp.bfloat16)  63.9 us
    psum x2, blocking collectives, coarse_step(): coarse = lax.psum(partial_coarse, ('crow', 'ccol')).astype(jnp.bfloat16)  61.2 us
    all_gather x2, blocking collectives, apply_stiffness(): lax.all_gather(rounded, ('crow', 'ccol'), axis=1, tiled=True)  54.3 us
    all_to_all x1, blocking collectives, gather_from_all(): lax.all_to_all(jnp.tile(shard, repeats), axis, split_axis=dim, concat_axi...  47.2 us
    scatter x2, local copies, waits for them, and re-layouts, coarse_step(): ordered = jnp.zeros((block_width + 1, case_count), jnp.bfloat16).at[arriv...  31.8 us
  transfers between devices with their start and end apart: 9, of which 8 were waited for; matrix products, arithmetic and copies ran while one was open for 0% of the time, Pallas kernels for 0%

profile of v1, /device:TPU:6, one launch (start us, length us, event | category | flops | bytes accessed | tf_op | source)
XLA Modules:
  0.0 936.9 jit_solution(3190025851106216787)
XLA Ops:
  7.2 1.0 convolution_bitcast_fusion.4
  8.2 33.6 %psum.42 = bf16[2,48,128]{2,1,0:T(8,128)(2,1)S(1)} all-reduce(f32[2,48,128]{2,1,0:T(8,128)S(1)} %convolution_bitcast_fusion.4), channel_id=1, replica_groups=mesh['sub'=64,'crow'=4,'ccol'=2] {'crow','ccol'}, use_global_device_ids=true, to_apply=%region_0.0 | all-reduce | flops 12288 | bytes 73728 | tf_op jit(solution)/shard_map/psum | solution.py:85
  41.9 1.4 tile.17
  43.2 13.4 %all-to-all-start = ((bf16[64,96,128]{2,1,0:T(8,128)(2,1)}), bf16[64,96,128]{2,1,0:T(8,128)(2,1)S(1)}, u32[]{:S(2)}, u32[]{:S(2)}) async-start(bf16[64,96,128]{2,1,0:T(8,128)(2,1)} %tile.17), calls=%async_computation | async-start | bytes 3145728 | tf_op jit(solution)/shard_map/all_to_all | solution.py:10
  56.8 1.3 dynamic-slice
  59.0 300.7 %all-reduce = s32[6144]{0:T(1024)S(1)} all-reduce(s32[6144]{0:T(1024)S(1)} %dynamic-update-slice), channel_id=1, replica_groups=mesh['sub'=64,'crow'=4,'ccol'=2] {'sub'}, use_global_device_ids=true, to_apply=%add | all-reduce | flops 6144 | bytes 49152
  359.7 15.9 %scatter_custom_fusion = bf16[769,128]{1,0:T(8,128)(2,1)S(1)} fusion(s32[6144]{0:T(1024)S(1)} %compare_select_fusion, bf16[6144,128]{1,0:T(8,128)(2,1)S(1)} %bitcast.68, bf16[]{:T(256)} %constant.10.clone.1), kind=kCustom, calls=%fused_computation.46 | custom fusion | bytes 196866 | tf_op jit(solution)/shard_map/scatter | solution.py:72
  375.8 31.7 %psum.43 = bf16[96,128]{1,0:T(8,128)(2,1)} all-reduce(f32[96,128]{1,0:T(8,128)S(1)} %convolution_bitcast_fusion.3), channel_id=1, replica_groups=mesh['sub'=64,'crow'=4,'ccol'=2] {'crow','ccol'}, use_global_device_ids=true, to_apply=%region_2.3 | all-reduce | flops 12288 | bytes 73728 | tf_op jit(solution)/shard_map/psum | solution.py:75
  407.6 78.8 %all-gather.3.cloned.1.call-done = bf16[6144,128]{1,0:T(8,128)(2,1)} async-done(((bf16[96,128]{1,0:T(8,128)(2,1)}), bf16[6144,128]{1,0:T(8,128)(2,1)}) %all-gather.3.cloned.1.call-update) | async-done | bytes 1572880 | tf_op jit(solution)/shard_map/all_gather | solution.py:76
  486.5 2.2 gather_fusion
  489.9 27.2 %all_gather.21 = bf16[2,1024,128]{2,1,0:T(8,128)(2,1)S(1)} all-gather(bf16[2,128,128]{2,1,0:T(8,128)(2,1)S(1)} %get-tuple-element.6), channel_id=1, replica_groups=mesh['sub'=64,'crow'=4,'ccol'=2] {'crow','ccol'}, dimensions={1}, use_global_device_ids=true | all-gather | bytes 589824 | tf_op jit(solution)/shard_map/all_gather | solution.py:36
  518.7 65.4 %all-reduce.4.cloned.1.call-done = bf16[2,2,128,128]{3,2,0,1:T(8,128)(2,1)} async-done(((bf16[2,2,128,128]{3,2,0,1:T(8,128)(2,1)}), bf16[2,2,128,128]{3,2,0,1:T(8,128)(2,1)}) %all-reduce.4.cloned.1.call-update) | async-done | bytes 131088 | tf_op jit(solution)/shard_map/psum | solution.py:43
  585.0 8.1 collective-permute-start.1
  593.1 1.9 collective-permute-start
  595.2 1.0 fusion.14
  596.2 6.5 collective-permute-done
  602.7 1.0 fusion.6
  604.4 30.3 %psum.45 = bf16[2,48,128]{2,1,0:T(8,128)(2,1)S(1)} all-reduce(f32[2,48,128]{2,1,0:T(8,128)S(1)} %convolution_bitcast_fusion.2), channel_id=1, replica_groups=mesh['sub'=64,'crow'=4,'ccol'=2] {'crow','ccol'}, use_global_device_ids=true, to_apply=%region_4.5 | all-reduce | flops 12288 | bytes 73728 | tf_op jit(solution)/shard_map/psum | solution.py:85
  634.9 47.2 %all_to_all.18 = bf16[64,96,128]{2,1,0:T(8,128)(2,1)S(1)} all-to-all(bf16[64,96,128]{2,1,0:T(8,128)(2,1)S(1)} %tile.19), channel_id=1, replica_groups=mesh['sub'=64,'crow'=4,'ccol'=2] {'sub'}, dimensions={0} | all-to-all | bytes 3145728 | tf_op jit(solution)/shard_map/all_to_all | solution.py:10
  682.1 15.9 %scatter_custom_fusion.1 = bf16[769,128]{1,0:T(8,128)(2,1)S(1)} fusion(s32[6144]{0:T(1024)S(1)} %compare_select_fusion, bf16[6144,128]{1,0:T(8,128)(2,1)S(1)} %bitcast.69, bf16[]{:T(256)} %constant.10.clone.1), kind=kCustom, calls=%fused_computation.44 | custom fusion | bytes 196866 | tf_op jit(solution)/shard_map/scatter | solution.py:72
  698.2 29.6 %psum.46 = bf16[96,128]{1,0:T(8,128)(2,1)} all-reduce(f32[96,128]{1,0:T(8,128)S(1)} %convolution_bitcast_fusion.1), channel_id=1, replica_groups=mesh['sub'=64,'crow'=4,'ccol'=2] {'crow','ccol'}, use_global_device_ids=true, to_apply=%region_6.7 | all-reduce | flops 12288 | bytes 73728 | tf_op jit(solution)/shard_map/psum | solution.py:75
  727.8 27.4 %all_gather.22 = bf16[2,1024,128]{2,1,0:T(8,128)(2,1)S(1)} all-gather(bf16[2,128,128]{2,1,0:T(8,128)(2,1)} %copy-done.4), channel_id=1, replica_groups=mesh['sub'=64,'crow'=4,'ccol'=2] {'crow','ccol'}, dimensions={1}, use_global_device_ids=true | all-gather | bytes 589824 | tf_op jit(solution)/shard_map/all_gather | solution.py:116
  755.3 57.2 %all-gather.5.cloned.1.call-done = bf16[6144,128]{1,0:T(8,128)(2,1)} async-done(((bf16[96,128]{1,0:T(8,128)(2,1)}), bf16[6144,128]{1,0:T(8,128)(2,1)}) %all-gather.5.cloned.1.call-update) | async-done | bytes 1572880 | tf_op jit(solution)/shard_map/all_gather | solution.py:76
  812.4 2.4 gather_fusion.1
  815.0 1.0 fusion.65
  816.0 27.2 %all_gather.24 = bf16[2,1024,128]{2,1,0:T(8,128)(2,1)S(1)} all-gather(bf16[2,128,128]{2,1,0:T(8,128)(2,1)S(1)} %get-tuple-element.8), channel_id=1, replica_groups=mesh['sub'=64,'crow'=4,'ccol'=2] {'crow','ccol'}, dimensions={1}, use_global_device_ids=true | all-gather | bytes 589824 | tf_op jit(solution)/shard_map/all_gather | solution.py:36
  844.7 65.4 %all-reduce.6.cloned.1.call-done = bf16[2,2,128,128]{3,2,0,1:T(8,128)(2,1)} async-done(((bf16[2,2,128,128]{3,2,0,1:T(8,128)(2,1)}), bf16[2,2,128,128]{3,2,0,1:T(8,128)(2,1)}) %all-reduce.6.cloned.1.call-update) | async-done | bytes 131088 | tf_op jit(solution)/shard_map/psum | solution.py:43
  911.0 8.1 collective-permute-start.3
  919.2 1.9 collective-permute-start.2
  921.3 1.0 fusion.11
  922.2 6.5 collective-permute-done.2
  928.7 1.6 fusion.3
  (58 shorter events, 8.7 us)
Async XLA Ops:
  7.2 481.8 %copy-start = (bf16[2,128,1024]{2,1,0:T(8,128)(2,1)S(1)}, bf16[2,128,1024]{2,1,0:T(8,128)(2,1)}, u32[]{:S(2)}) copy-start(bf16[2,128,1024]{2,1,0:T(8,128)(2,1)} %param.10) | copy-start | bytes 1572868
  43.2 13.5 %copy-start.10 = (s32[2,48]{1,0:T(2,128)S(1)}, s32[2,48]{1,0:T(2,128)}, u32[]{:S(2)}) copy-start(s32[2,48]{1,0:T(2,128)} %param.13) | copy-start | bytes 1156
  43.2 332.4 %copy-start.3 = (bf16[96,768]{1,0:T(8,128)(2,1)S(1)}, bf16[96,768]{1,0:T(8,128)(2,1)}, u32[]{:S(2)}) copy-start(bf16[96,768]{1,0:T(8,128)(2,1)} %param.12) | copy-start | bytes 442372
  43.2 445.5 %copy-start.6 = (bf16[2,128,48]{1,2,0:T(8,128)(2,1)S(1)}, bf16[2,128,48]{1,2,0:T(8,128)(2,1)}, u32[]{:S(2)}) copy-start(bf16[2,128,48]{1,2,0:T(8,128)(2,1)} %param.11) | copy-start | bytes 73732
  43.2 445.7 %copy-start.2 = (bf16[2,1024,128]{2,1,0:T(8,128)(2,1)S(1)}, bf16[2,1024,128]{2,1,0:T(8,128)(2,1)}, u32[]{:S(2)}) copy-start(bf16[2,1024,128]{2,1,0:T(8,128)(2,1)} %param.8) | copy-start | bytes 1572868
  43.2 316.5 %all-to-all-start = ((bf16[64,96,128]{2,1,0:T(8,128)(2,1)}), bf16[64,96,128]{2,1,0:T(8,128)(2,1)S(1)}, u32[]{:S(2)}, u32[]{:S(2)}) async-start(bf16[64,96,128]{2,1,0:T(8,128)(2,1)} %tile.17), calls=%async_computation | async-start | bytes 3145728 | tf_op jit(solution)/shard_map/all_to_all | solution.py:10
  56.6 429.8 %all-gather.3.cloned.1.call-start = ((), (), s32[]{:S(2)}) async-start(), calls=%async_computation.2 | async-start | bytes 1597440 | tf_op jit(solution)/shard_map/all_gather | solution.py:76
  359.7 157.4 %copy-start.1 = (bf16[2,128,1024]{2,1,0:T(8,128)(2,1)S(1)}, bf16[2,128,1024]{2,1,0:T(8,128)(2,1)}, u32[]{:S(2)}) copy-start(bf16[2,128,1024]{2,1,0:T(8,128)(2,1)} %param.9) | copy-start | bytes 1572868
  407.5 176.6 %all-reduce.4.cloned.1.call-start = ((), (), s32[]{:S(2)}) async-start(), calls=%async_computation.3 | async-start | bytes 262144 | tf_op jit(solution)/shard_map/psum | solution.py:43
  407.6 82.3 %copy-start.9 = (s32[1024]{0:T(1024)}, s32[1024]{0:T(1024)S(1)}, u32[]{:S(2)}) copy-start(s32[1024]{0:T(1024)S(1)} %pad_clamp_fusion) | copy-start | bytes 12292
  488.9 28.4 %copy-start.7 = (s32[2,128]{1,0:T(2,128)S(1)}, s32[2,128]{1,0:T(2,128)}, u32[]{:S(2)}) copy-start(s32[2,128]{1,0:T(2,128)} %param.15) | copy-start | bytes 3076
  488.9 28.7 %copy-start.8 = (s32[2,128]{1,0:T(2,128)S(1)}, s32[2,128]{1,0:T(2,128)}, u32[]{:S(2)}) copy-start(s32[2,128]{1,0:T(2,128)} %param.14) | copy-start | bytes 3076
  518.7 293.8 %all-gather.5.cloned.1.call-start = ((), (), s32[]{:S(2)}) async-start(), calls=%async_computation.4 | async-start | bytes 1597440 | tf_op jit(solution)/shard_map/all_gather | solution.py:76
  585.0 10.3 %collective-permute-start.1 = (bf16[1,2,128,128]{3,2,0,1:T(8,128)(2,1)S(1)}, bf16[1,2,128,128]{3,2,0,1:T(8,128)(2,1)S(1)}, u32[]{:S(2)}, u32[]{:S(2)}) collective-permute-start(bf16[1,2,128,128]{3,2,0,1:T(8,128)(2,1)S(1)} %get-tuple-element.5), channel_id=1, source_target_pairs={{8,0},{16,8},{24,16},{32,24},{40,32},{48,40},{56,48},{64,56},{72,6... | collective-permute-start | bytes 196616 | tf_op jit(solution)/shard_map/ppermute | solution.py:24
  593.1 9.6 %collective-permute-start = (bf16[1,2,128,128]{3,2,0,1:T(8,128)(2,1)S(1)}, bf16[1,2,128,128]{3,2,0,1:T(8,128)(2,1)S(1)}, u32[]{:S(2)}, u32[]{:S(2)}) collective-permute-start(bf16[1,2,128,128]{3,2,0,1:T(8,128)(2,1)S(1)} %get-tuple-element.4), channel_id=1, source_target_pairs={{0,8},{8,16},{16,24},{24,32},{32,40},{40,48},{48,56},{56,64},{64,7... | collective-permute-start | bytes 196616 | tf_op jit(solution)/shard_map/ppermute | solution.py:21
  603.6 0.6 copy-start.4
  698.0 117.0 %copy-start.5 = (f32[2,128,128]{2,1,0:T(8,128)S(1)}, f32[2,128,128]{2,1,0:T(8,128)}, u32[]{:S(2)}) copy-start(f32[2,128,128]{2,1,0:T(8,128)} %get-tuple-element.7) | copy-start | bytes 393220
  727.8 182.3 %all-reduce.6.cloned.1.call-start = ((), (), s32[]{:S(2)}) async-start(), calls=%async_computation.5 | async-start | bytes 262144 | tf_op jit(solution)/shard_map/psum | solution.py:43
  911.0 10.3 %collective-permute-start.3 = (bf16[1,2,128,128]{3,2,0,1:T(8,128)(2,1)S(1)}, bf16[1,2,128,128]{3,2,0,1:T(8,128)(2,1)S(1)}, u32[]{:S(2)}, u32[]{:S(2)}) collective-permute-start(bf16[1,2,128,128]{3,2,0,1:T(8,128)(2,1)S(1)} %get-tuple-element.3), channel_id=1, source_target_pairs={{8,0},{16,8},{24,16},{32,24},{40,32},{48,40},{56,48},{64,56},{72,6... | collective-permute-start | bytes 196616 | tf_op jit(solution)/shard_map/ppermute | solution.py:24
  919.2 9.6 %collective-permute-start.2 = (bf16[1,2,128,128]{3,2,0,1:T(8,128)(2,1)S(1)}, bf16[1,2,128,128]{3,2,0,1:T(8,128)(2,1)S(1)}, u32[]{:S(2)}, u32[]{:S(2)}) collective-permute-start(bf16[1,2,128,128]{3,2,0,1:T(8,128)(2,1)S(1)} %get-tuple-element.2), channel_id=1, source_target_pairs={{0,8},{8,16},{16,24},{24,32},{32,40},{40,48},{48,56},{56,64},{64,7... | collective-permute-start | bytes 196616 | tf_op jit(solution)/shard_map/ppermute | solution.py:21
Sparse Core Ops, SparseCore 0:
  407.6 78.8 all-gather.2
  518.8 65.2 all-reduce.3
  727.9 84.4 all-gather.4
  844.8 65.2 all-reduce.5
